TPU v7x, 32 devices: a whole 2x2x4 slice. The times are simulated.
32 devices in a mesh: dp: 4 (over z), tensor: 2 (over x), expert: 4 (over y, core).
Axes of the slice: x: 2, y: 2, z: 4, core: 2. Of those that a mesh axis runs over, the one named last changes fastest.
Arguments:
- block_in: bfloat16 [4096, 2048], P(('dp', 'expert'), 'tensor')
- route_ids: int32 [4096, 8], P(('dp', 'expert')), may hold values from 0 to 31, as said below
- route_weights: float32 [4096, 8], P(('dp', 'expert')), may hold values from 0.04 to 0.3
- cotangent: bfloat16 [4096, 2048], P(('dp', 'expert'), 'tensor'), may hold values from -6 to 6
- attention_gain: bfloat16 [2048], P('dp'), may hold values from 0.5 to 1.5
- query_weight: bfloat16 [2048, 4096], P('dp', 'tensor'), may hold values from -0.125 to 0.125
- key_projection_matrix: bfloat16 [2048, 512], P('dp', 'tensor'), may hold values from -0.125 to 0.125
- value_projection_matrix: bfloat16 [2048, 512], P('dp', 'tensor'), may hold values from -0.125 to 0.125
- output_weight: bfloat16 [2048, 4096], P('dp', 'tensor'), may hold values from -0.75 to 0.75
- query_gain: bfloat16 [128], P('dp'), may hold values from 0.5 to 1.5
- key_gain: bfloat16 [128], P('dp'), may hold values from 0.5 to 1.5
- expert_gain: bfloat16 [2048], P('dp'), may hold values from 0.5 to 1.5
- expert_gate_matrix: bfloat16 [32, 2048, 768], P(('dp', 'expert'), None, 'tensor'), may hold values from -0.125 to 0.125
- expert_up_matrix: bfloat16 [32, 2048, 768], P(('dp', 'expert'), None, 'tensor'), may hold values from -0.125 to 0.125
- expert_down_matrix: bfloat16 [32, 768, 2048], P(('dp', 'expert'), 'tensor'), may hold values from -0.625 to 0.625
Outputs:
- block_out: bfloat16 [4096, 2048], P(('dp', 'expert'), 'tensor')
- block_in_grad: float32 [4096, 2048], P(('dp', 'expert'), 'tensor')
- attention_gain_grad: float32 [2048], P('dp')
- query_weight_grad: float32 [2048, 4096], P('dp', 'tensor')
- key_weight_grad: float32 [2048, 512], P('dp', 'tensor')
- value_weight_grad: float32 [2048, 512], P('dp', 'tensor')
- output_weight_grad: float32 [2048, 4096], P('dp', 'tensor')
- query_gain_grad: float32 [128], P('dp')
- key_gain_grad: float32 [128], P('dp')
- expert_gain_grad: float32 [2048], P('dp')
- gate_grad: float32 [32, 2048, 768], P(('dp', 'expert'), None, 'tensor')
- up_matrix_gradient: float32 [32, 2048, 768], P(('dp', 'expert'), None, 'tensor')
- down_grad: float32 [32, 768, 2048], P(('dp', 'expert'), 'tensor')
Inputs may be any that keep to these rules, and one draw needn't show every extreme that they name: `route_ids`: each row names 8 different experts. Among the 256 rows of one device (aligned blocks of rows), no expert is named by more than 128 rows, and in every draw some expert is named by exactly 128 rows in every block.
All inputs are finite; a program needn't handle non-finite values.
Results may differ from a plain program's by a relative error of at most 0.025.
Values may be sent and summed in bfloat16 or wider, within the bound.
No kernel may reach another device: no remote copies, remote signals or barrier semaphores. Data moves between devices by JAX's collectives and lax.ppermute only.
A program may use at most 384 MiB of HBM per device.

v0:
```python
import math

import jax
import jax.numpy as jnp
from jax import lax
from jax.sharding import PartitionSpec as P

HEAD_SIZE = 128
SEQ = 256


epsilon = 1e-06
rope_base = 1000000.0


def rope_tables(positions):
    half_dim = HEAD_SIZE // 2
    frequency = rope_base ** (-(jnp.arange(half_dim, dtype=jnp.float32) * 2.0) / HEAD_SIZE)
    angles = positions.astype(jnp.float32)[:, None] * frequency[None, :]
    angles = jnp.concatenate([angles, angles], axis=1)
    return (jnp.cos(angles)[:, None, :], jnp.sin(angles)[:, None, :])


def prepare(values, scales, cosine, sine_table, factor):
    mean_sq = jnp.mean(values * values, axis=-1, keepdims=True)
    normed = values * lax.rsqrt(mean_sq + epsilon) * scales
    half_dim = values.shape[-1] // 2
    turned = jnp.concatenate([-normed[..., half_dim:], normed[..., :half_dim]], axis=-1)
    return (normed * cosine + turned * sine_table) * factor


def dot_last(first_arr, second_arr):
    return lax.dot_general(
        first_arr, second_arr, (((1,), (1,)), ((), ())), preferred_element_type=jnp.float32
    )


def dot_first(first_arr, second_arr):
    return lax.dot_general(
        first_arr, second_arr, (((0,), (0,)), ((), ())), preferred_element_type=jnp.float32
    )


def route_rows(buffer):
    return lax.all_to_all(buffer, ("dp", "expert"), split_axis=1, concat_axis=1, tiled=True)


def dispatch_rows(send_full, local_experts, group_devices, capacity):
    model_width = send_full.shape[1]
    shaped = send_full.reshape(local_experts, group_devices, capacity, model_width)
    whole = route_rows(shaped)
    return whole.reshape(local_experts, group_devices * capacity, model_width)


def local(
    block_in,
    route_ids,
    route_weights,
    cotangent,
    attention_gain,
    query_weight,
    key_projection_matrix,
    value_projection_matrix,
    output_weight,
    query_gain,
    key_gain,
    expert_gain,
    expert_gate_matrix,
    expert_up_matrix,
    expert_down_matrix,
):
    row_count = block_in.shape[0]
    full_in = lax.all_gather(block_in, "tensor", axis=1, tiled=True)
    gathered = (
        lax.all_gather(query_weight, "dp", axis=0, tiled=True),
        lax.all_gather(key_projection_matrix, "dp", axis=0, tiled=True),
        lax.all_gather(value_projection_matrix, "dp", axis=0, tiled=True),
        lax.all_gather(output_weight, "dp", axis=0, tiled=True),
        lax.all_gather(attention_gain, "dp", axis=0, tiled=True),
        lax.all_gather(query_gain, "dp", axis=0, tiled=True),
        lax.all_gather(key_gain, "dp", axis=0, tiled=True),
        lax.all_gather(expert_gain, "dp", axis=0, tiled=True),
    )
    query_full, key_full, value_full, output_full = (
        gathered[0],
        gathered[1],
        gathered[2],
        gathered[3],
    )
    norm_first = gathered[4].astype(jnp.float32)
    query_scale = gathered[5].astype(jnp.float32)
    key_scale = gathered[6].astype(jnp.float32)
    norm_second = gathered[7].astype(jnp.float32)
    model_width = full_in.shape[1]
    half_width = model_width // lax.axis_size("tensor")
    offset = lax.axis_index("tensor") * half_width
    input_float = full_in.astype(jnp.float32)
    inv_first = lax.rsqrt(jnp.mean(input_float * input_float, axis=1, keepdims=True) + epsilon)
    input_hat = input_float * inv_first
    normed = (input_hat * norm_first).astype(jnp.bfloat16)
    heads_local = query_full.shape[1] // HEAD_SIZE
    key_heads = key_full.shape[1] // HEAD_SIZE
    group_size = heads_local // key_heads
    seq_count = row_count // SEQ
    queries = jnp.dot(normed, query_full, preferred_element_type=jnp.float32).reshape(
        row_count, heads_local, HEAD_SIZE
    )
    key_rows = jnp.dot(normed, key_full, preferred_element_type=jnp.float32).reshape(
        row_count, key_heads, HEAD_SIZE
    )
    value_rows = jnp.dot(normed, value_full, preferred_element_type=jnp.float32).astype(
        jnp.bfloat16
    )
    positions = jnp.arange(row_count, dtype=jnp.int32) % SEQ
    cosine, sine_table = rope_tables(positions)
    factor = 1.0 / math.sqrt(HEAD_SIZE)
    query_rot = prepare(queries, query_scale, cosine, sine_table, factor).astype(jnp.bfloat16)
    key_rot = prepare(key_rows, key_scale, cosine, sine_table, 1.0).astype(jnp.bfloat16)
    query_seq = query_rot.reshape(seq_count, SEQ, key_heads, group_size, HEAD_SIZE)
    key_seq = key_rot.reshape(seq_count, SEQ, key_heads, HEAD_SIZE)
    value_seq = value_rows.reshape(seq_count, SEQ, key_heads, HEAD_SIZE)
    causal = jnp.arange(SEQ)[None, :] <= jnp.arange(SEQ)[:, None]
    scores = jnp.einsum("nqhgd,nkhd->nhgqk", query_seq, key_seq, preferred_element_type=jnp.float32)
    log_total = jnp.log(jnp.sum(jnp.where(causal, jnp.exp(scores), 0.0), axis=-1))
    soft_weights = jnp.where(causal, jnp.exp(scores - log_total[..., None]), 0.0)
    prob_half = soft_weights.astype(jnp.bfloat16)
    attended = (
        jnp.einsum("nhgqk,nkhd->nqhgd", prob_half, value_seq, preferred_element_type=jnp.float32)
        .astype(jnp.bfloat16)
        .reshape(row_count, heads_local * HEAD_SIZE)
    )
    partial_out = dot_last(attended, output_full)
    head_total = lax.psum(partial_out, "tensor")
    residual = input_float + head_total
    inv_second = lax.rsqrt(jnp.mean(residual * residual, axis=1, keepdims=True) + epsilon)
    resid_hat = residual * inv_second
    expert_in = (resid_hat * norm_second).astype(jnp.bfloat16)
    local_experts = expert_gate_matrix.shape[0]
    group_devices = lax.axis_size(("dp", "expert"))
    expert_total = local_experts * group_devices
    top_count = route_ids.shape[1]
    capacity = 2 * row_count * top_count // expert_total
    hit_counts = jnp.sum(
        (route_ids[:, :, None] == jnp.arange(expert_total, dtype=jnp.int32)[None, None, :]).astype(
            jnp.int32
        ),
        axis=1,
    )
    earlier = jnp.cumsum(hit_counts, axis=0) - hit_counts
    position = jnp.take_along_axis(earlier, route_ids, axis=1)
    slot_index = (
        route_ids % local_experts * group_devices + route_ids // local_experts
    ) * capacity + position
    slot_total = expert_total * capacity
    entry_count = row_count * top_count
    source_entry = (
        jnp.full((slot_total,), entry_count, jnp.int32)
        .at[slot_index.reshape(-1)]
        .set(jnp.arange(entry_count, dtype=jnp.int32))
    )
    source_row = source_entry // top_count
    weight_pad = jnp.concatenate([route_weights.reshape(-1), jnp.zeros((1,), jnp.float32)])
    slot_weight = jnp.take(weight_pad, source_entry)
    expert_pad = jnp.concatenate([expert_in, jnp.zeros((1, model_width), jnp.bfloat16)], axis=0)
    send_rows = jnp.take(expert_pad, source_row, axis=0)
    rows_per_expert = dispatch_rows(send_rows, local_experts, group_devices, capacity)
    gate_pre = jnp.einsum(
        "yun,yng->yug", rows_per_expert, expert_gate_matrix, preferred_element_type=jnp.float32
    )
    up_projected = jnp.einsum(
        "yun,yng->yug", rows_per_expert, expert_up_matrix, preferred_element_type=jnp.float32
    )
    sigmoid = jax.nn.sigmoid(gate_pre)
    swish_act = gate_pre * sigmoid
    swish_product = (swish_act * up_projected).astype(jnp.bfloat16)
    expert_out = jnp.einsum(
        "hri,hin->hrn", swish_product, expert_down_matrix, preferred_element_type=jnp.float32
    ).astype(jnp.bfloat16)
    returned = route_rows(
        expert_out.reshape(local_experts, group_devices, capacity, model_width)
    ).reshape(slot_total, model_width)
    combined = jnp.zeros((row_count, model_width), jnp.float32)
    for slot_rank in range(top_count):
        combined = combined + route_weights[:, slot_rank : slot_rank + 1] * jnp.take(
            returned, slot_index[:, slot_rank], axis=0
        ).astype(jnp.float32)
    mixture_half = lax.psum_scatter(
        combined.astype(jnp.bfloat16), "tensor", scatter_dimension=1, tiled=True
    ).astype(jnp.float32)
    resid_half = lax.dynamic_slice_in_dim(residual, offset, half_width, 1)
    block_out = (resid_half + mixture_half).astype(jnp.bfloat16)
    grad_full = lax.all_gather(cotangent, "tensor", axis=1, tiled=True)
    grad_float = grad_full.astype(jnp.float32)
    grad_pad = jnp.concatenate([grad_float, jnp.zeros((1, model_width), jnp.float32)], axis=0)
    send_grads = (slot_weight[:, None] * jnp.take(grad_pad, source_row, axis=0)).astype(
        jnp.bfloat16
    )
    slot_output_gradient = dispatch_rows(send_grads, local_experts, group_devices, capacity)
    act_grad = jnp.einsum(
        "qiy,qjy->qij", slot_output_gradient, expert_down_matrix, preferred_element_type=jnp.float32
    )
    gate_pre_gradient = (
        act_grad * up_projected * sigmoid * (1.0 + gate_pre * (1.0 - sigmoid))
    ).astype(jnp.bfloat16)
    up_pre_gradient = (act_grad * swish_act).astype(jnp.bfloat16)
    down_grad = jnp.einsum(
        "oxz,oxu->ozu", swish_product, slot_output_gradient, preferred_element_type=jnp.float32
    )
    gate_grad = jnp.einsum(
        "qxo,qxn->qon", rows_per_expert, gate_pre_gradient, preferred_element_type=jnp.float32
    )
    up_matrix_gradient = jnp.einsum(
        "qxo,qxn->qon", rows_per_expert, up_pre_gradient, preferred_element_type=jnp.float32
    )
    rows_back = jnp.einsum(
        "phn,pjn->phj", gate_pre_gradient, expert_gate_matrix, preferred_element_type=jnp.float32
    ) + jnp.einsum(
        "phn,pjn->phj", up_pre_gradient, expert_up_matrix, preferred_element_type=jnp.float32
    )
    returned_back = route_rows(
        rows_back.astype(jnp.bfloat16).reshape(local_experts, group_devices, capacity, model_width)
    ).reshape(slot_total, model_width)
    expert_in_part = jnp.zeros((row_count, model_width), jnp.float32)
    for slot_rank in range(top_count):
        expert_in_part = expert_in_part + jnp.take(
            returned_back, slot_index[:, slot_rank], axis=0
        ).astype(jnp.float32)
    expert_in_grad = lax.psum(expert_in_part, "tensor")
    scaled = expert_in_grad * norm_second
    resid_grad = grad_float + inv_second * (
        scaled - resid_hat * jnp.mean(scaled * resid_hat, axis=1, keepdims=True)
    )
    expert_gain_part = jnp.sum(expert_in_grad * resid_hat, axis=0)
    resid_cast = resid_grad.astype(jnp.bfloat16)
    attended_grad = jnp.dot(resid_cast, output_full, preferred_element_type=jnp.float32).astype(
        jnp.bfloat16
    )
    scores_again = jnp.einsum(
        "nqhgd,nkhd->nhgqk", query_seq, key_seq, preferred_element_type=jnp.float32
    )
    probs_again = jnp.where(causal, jnp.exp(scores_again - log_total[..., None]), 0.0)
    probs_again_half = probs_again.astype(jnp.bfloat16)
    grad_seq = attended_grad.reshape(seq_count, SEQ, key_heads, group_size, HEAD_SIZE)
    value_grad = (
        jnp.einsum(
            "nhgqk,nqhgd->nkhd", probs_again_half, grad_seq, preferred_element_type=jnp.float32
        )
        .astype(jnp.bfloat16)
        .reshape(row_count, key_heads * HEAD_SIZE)
    )
    prob_grad = jnp.einsum(
        "nqhgd,nkhd->nhgqk", grad_seq, value_seq, preferred_element_type=jnp.float32
    )
    row_inner = jnp.sum(probs_again * prob_grad, axis=-1, keepdims=True)
    score_grad = (probs_again * (prob_grad - row_inner)).astype(jnp.bfloat16)
    query_rot_grad = jnp.einsum(
        "nhgqk,nkhd->nqhgd", score_grad, key_seq, preferred_element_type=jnp.float32
    ).reshape(row_count, heads_local, HEAD_SIZE)
    key_rot_grad = jnp.einsum(
        "nhgqk,nqhgd->nkhd", score_grad, query_seq, preferred_element_type=jnp.float32
    ).reshape(row_count, key_heads, HEAD_SIZE)
    _, query_pull = jax.vjp(
        lambda values, scales: prepare(values, scales, cosine, sine_table, factor),
        queries,
        query_scale,
    )
    query_grad, query_scale_grad = query_pull(query_rot_grad)
    _, key_pull = jax.vjp(
        lambda values, scales: prepare(values, scales, cosine, sine_table, 1.0), key_rows, key_scale
    )
    key_grad, key_scale_grad = key_pull(key_rot_grad)
    query_cast = query_grad.reshape(row_count, heads_local * HEAD_SIZE).astype(jnp.bfloat16)
    key_cast = key_grad.reshape(row_count, key_heads * HEAD_SIZE).astype(jnp.bfloat16)
    normed_part = (
        dot_last(query_cast, query_full)
        + dot_last(key_cast, key_full)
        + dot_last(value_grad, value_full)
    )
    normed_grad, query_scale_sum, key_scale_sum = (
        lax.psum(normed_part.astype(jnp.bfloat16), "tensor").astype(jnp.float32),
        lax.psum(query_scale_grad.astype(jnp.bfloat16), "tensor").astype(jnp.float32),
        lax.psum(key_scale_grad.astype(jnp.bfloat16), "tensor").astype(jnp.float32),
    )
    scaled_first = normed_grad * norm_first
    input_grad = resid_grad + inv_first * (
        scaled_first - input_hat * jnp.mean(scaled_first * input_hat, axis=1, keepdims=True)
    )
    attention_gain_part = jnp.sum(normed_grad * input_hat, axis=0)
    block_in_grad = lax.dynamic_slice_in_dim(input_grad, offset, half_width, 1)
    grad_terms = (
        dot_first(normed, query_cast),
        dot_first(normed, key_cast),
        dot_first(normed, value_grad),
        dot_first(resid_cast, attended),
        attention_gain_part,
        query_scale_sum,
        key_scale_sum,
        expert_gain_part,
    )
    pieces = (
        lax.psum_scatter(
            grad_terms[0].astype(jnp.bfloat16), "dp", scatter_dimension=0, tiled=True
        ).astype(jnp.float32),
        lax.psum_scatter(
            grad_terms[1].astype(jnp.bfloat16), "dp", scatter_dimension=0, tiled=True
        ).astype(jnp.float32),
        lax.psum_scatter(
            grad_terms[2].astype(jnp.bfloat16), "dp", scatter_dimension=0, tiled=True
        ).astype(jnp.float32),
        lax.psum_scatter(
            grad_terms[3].astype(jnp.bfloat16), "dp", scatter_dimension=0, tiled=True
        ).astype(jnp.float32),
        lax.psum_scatter(
            grad_terms[4].astype(jnp.bfloat16), "dp", scatter_dimension=0, tiled=True
        ).astype(jnp.float32),
        lax.psum_scatter(
            grad_terms[5].astype(jnp.bfloat16), "dp", scatter_dimension=0, tiled=True
        ).astype(jnp.float32),
        lax.psum_scatter(
            grad_terms[6].astype(jnp.bfloat16), "dp", scatter_dimension=0, tiled=True
        ).astype(jnp.float32),
        lax.psum_scatter(
            grad_terms[7].astype(jnp.bfloat16), "dp", scatter_dimension=0, tiled=True
        ).astype(jnp.float32),
    )
    reduced = (
        lax.psum(pieces[0].astype(jnp.bfloat16), "expert").astype(jnp.float32),
        lax.psum(pieces[1].astype(jnp.bfloat16), "expert").astype(jnp.float32),
        lax.psum(pieces[2].astype(jnp.bfloat16), "expert").astype(jnp.float32),
        lax.psum(pieces[3].astype(jnp.bfloat16), "expert").astype(jnp.float32),
        lax.psum(pieces[4].astype(jnp.bfloat16), "expert").astype(jnp.float32),
        lax.psum(pieces[5].astype(jnp.bfloat16), "expert").astype(jnp.float32),
        lax.psum(pieces[6].astype(jnp.bfloat16), "expert").astype(jnp.float32),
        lax.psum(pieces[7].astype(jnp.bfloat16), "expert").astype(jnp.float32),
    )
    return (
        block_out,
        block_in_grad,
        reduced[4],
        reduced[0],
        reduced[1],
        reduced[2],
        reduced[3],
        reduced[5],
        reduced[6],
        reduced[7],
        gate_grad,
        up_matrix_gradient,
        down_grad,
    )


def solution(mesh):
    placed = (
        P(("dp", "expert"), "tensor"),
        P(("dp", "expert"), None),
        P(("dp", "expert"), None),
        P(("dp", "expert"), "tensor"),
        P("dp"),
        P("dp", "tensor"),
        P("dp", "tensor"),
        P("dp", "tensor"),
        P("dp", "tensor"),
        P("dp"),
        P("dp"),
        P("dp"),
        P(("dp", "expert"), None, "tensor"),
        P(("dp", "expert"), None, "tensor"),
        P(("dp", "expert"), "tensor", None),
    )
    return jax.shard_map(
        local,
        mesh=mesh,
        in_specs=placed,
        out_specs=(
            P(("dp", "expert"), "tensor"),
            P(("dp", "expert"), "tensor"),
            P("dp"),
            P("dp", "tensor"),
            P("dp", "tensor"),
            P("dp", "tensor"),
            P("dp", "tensor"),
            P("dp"),
            P("dp"),
            P("dp"),
            P(("dp", "expert"), None, "tensor"),
            P(("dp", "expert"), None, "tensor"),
            P(("dp", "expert"), "tensor", None),
        ),
        check_vma=False,
    )
```

profile of v0, /device:TPU:0, one launch (start us, length us, event | category | flops | bytes accessed | tf_op | source)
XLA Modules:
  0.0 2912.9 jit_solution(6559735544885837621)
XLA Ops:
  12.8 13.6 gather_fusion.3
  35.7 23.0 gather_fusion.1
  61.6 33.3 %gather_fusion.2 = f32[4096,2048]{1,0:T(8,128)} fusion(f32[257,2048]{1,0:T(8,128)} %concatenate.43, s32[4096]{0:T(1024)S(1)} %get-tuple-element.60), kind=kCustom, calls=%fused_computation.18 | custom fusion | bytes 67125248 | tf_op jit(solution)/shard_map/jit(_take)/gather | solution.py:195
  94.9 18.1 fusion.1
  123.5 408.6 %all-reduce.15 = (bf16[128]{0:T(256)(128)(2,1)S(1)}, bf16[128]{0:T(256)(128)(2,1)S(1)}) all-reduce(bf16[128]{0:T(256)(128)(2,1)S(1)} %dynamic-update-slice, bf16[128]{0:T(256)(128)(2,1)S(1)} %dynamic-update-slice.1), channel_id=1, replica_groups=mesh['dp'=4,'tensor'=2,'expert'=4] {'dp'}, use_global_device_ids=true, to_apply=%add.6 | all-reduce | flops 256 | bytes 1024
  532.1 236.0 %all-gather = bf16[4,1,512]{2,1,0:T(2,128)(2,1)S(1)} all-gather(bf16[1,1,512]{2,1,0:T(2,128)(2,1)S(1)} %reshape.592), channel_id=1, replica_groups=mesh['dp'=4,'tensor'=2,'expert'=4] {'dp'}, dimensions={0}, use_global_device_ids=true | all-gather | bytes 5120 | tf_op jit(solution)/shard_map/all_gather | solution.py:79
  800.9 12.1 all-gather.1
  813.1 48.9 %all-reduce.22.cloned.1.call-done = f32[256,2048]{1,0:T(8,128)} async-done(((f32[256,2048]{1,0:T(8,128)}), f32[256,2048]{1,0:T(8,128)}) %all-reduce.22.cloned.1.call-update) | async-done | bytes 2097168 | tf_op jit(solution)/shard_map/psum | solution.py:133
  866.8 32.7 %gather_fusion = bf16[4096,2048]{1,0:T(8,128)(2,1)} fusion(bf16[257,2048]{1,0:T(8,128)(2,1)} %concatenate.41, s32[4096]{0:T(1024)S(1)} %get-tuple-element.60), kind=kCustom, calls=%fused_computation.16 | custom fusion | bytes 33570816 | tf_op jit(solution)/shard_map/jit(_take)/gather | solution.py:165
  899.5 14.1 copy_select_fusion.1
  919.3 14.1 copy.257
  933.5 282.5 %all-to-all-done = bf16[2,16,128,2048]{3,2,0,1:T(8,128)(2,1)} async-done(((bf16[2,16,128,2048]{3,2,0,1:T(8,128)(2,1)}), bf16[2,16,128,2048]{3,2,0,1:T(8,128)(2,1)}, u32[]{:S(2)}, u32[]{:S(2)}) %all-to-all-start) | async-done | bytes 16777248 | tf_op jit(solution)/shard_map/all_to_all | solution.py:45
  1246.3 19.8 multiply_convert_fusion
  1266.1 17.8 fusion.63
  1283.8 22.6 add_convert_fusion
  1306.5 14.1 copy.258
  1320.6 70.4 %all-to-all-start.3 = ((bf16[2,16,128,2048]{3,2,0,1:T(8,128)(2,1)}), bf16[2,16,128,2048]{3,2,0,1:T(8,128)(2,1)}, u32[]{:S(2)}, u32[]{:S(2)}) async-start(bf16[2,16,128,2048]{3,2,0,1:T(8,128)(2,1)} %copy.258), calls=%async_computation.4 | async-start | bytes 33554432 | tf_op jit(solution)/shard_map/all_to_all | solution.py:45
  1391.3 296.3 %all-to-all-done.3 = bf16[2,16,128,2048]{3,2,0,1:T(8,128)(2,1)} async-done(((bf16[2,16,128,2048]{3,2,0,1:T(8,128)(2,1)}), bf16[2,16,128,2048]{3,2,0,1:T(8,128)(2,1)}, u32[]{:S(2)}, u32[]{:S(2)}) %all-to-all-start.3) | async-done | bytes 16777248 | tf_op jit(solution)/shard_map/all_to_all | solution.py:45
  1687.6 14.5 copy.259
  1803.0 122.8 %all-reduce.24.cloned.1.call-done = f32[256,2048]{1,0:T(8,128)} async-done(((f32[256,2048]{1,0:T(8,128)}), f32[256,2048]{1,0:T(8,128)}) %all-reduce.24.cloned.1.call-update) | async-done | bytes 2097168 | tf_op jit(solution)/shard_map/psum | solution.py:228
  1959.0 14.4 convolution_convert_fusion
  1973.4 14.1 copy.252
  2007.5 424.6 %all-to-all-done.1 = bf16[2,16,128,2048]{3,2,0,1:T(8,128)(2,1)} async-done(((bf16[2,16,128,2048]{3,2,0,1:T(8,128)(2,1)}), bf16[2,16,128,2048]{3,2,0,1:T(8,128)(2,1)}, u32[]{:S(2)}, u32[]{:S(2)}) %all-to-all-start.1) | async-done | bytes 16777248 | tf_op jit(solution)/shard_map/all_to_all | solution.py:45
  2432.1 14.4 copy.253
  2543.6 15.4 fusion.67
  2567.7 15.3 fusion.66
  2583.0 24.6 reduce-scatter.8.cloned.1.call-done
  2607.7 12.9 fusion.68
  2620.6 134.7 %reduce-scatter.6.cloned.1.call-done = bf16[256,1024]{1,0:T(8,128)(2,1)} async-done(((bf16[256,2048]{1,0:T(8,128)(2,1)}), bf16[256,1024]{1,0:T(8,128)(2,1)}) %reduce-scatter.6.cloned.1.call-update) | async-done | bytes 524304 | tf_op jit(solution)/shard_map/reduce_scatter | solution.py:187
  2757.6 41.4 %all-reduce.26.cloned.1.call-done = bf16[256,2048]{1,0:T(8,128)(2,1)} async-done(((bf16[256,2048]{1,0:T(8,128)(2,1)}), bf16[256,2048]{1,0:T(8,128)(2,1)}) %all-reduce.26.cloned.1.call-update) | async-done | bytes 1048592 | tf_op jit(solution)/shard_map/psum | solution.py:280
  2803.3 12.1 all-reduce.14
  2832.5 63.2 %all-reduce.28.cloned.1.call-done = (bf16[512,2048]{1,0:T(8,128)(2,1)}, bf16[512,256]{1,0:T(8,128)(2,1)}, bf16[512,256]{1,0:T(8,128)(2,1)}, bf16[512,2048]{1,0:T(8,128)(2,1)}) async-done(((bf16[512,2048]{1,0:T(8,128)(2,1)}, bf16[512,256]{1,0:T(8,128)(2,1)}, bf16[512,256]{1,0:T(8,128)(2,1)}, bf16[512,2048]{1,0:T(8,128)(2,1)}), (bf16[512,2048]{1,0:T(8,128)(2,1)}, bf16[512,256]{1,0:T(8,128)(2,1)}, ...) | async-done | bytes 4718608 | tf_op jit(solution)/shard_map/psum | solution.py:327
  (357 shorter events, 392.7 us)
Async XLA Ops:
  7.2 1239.1 %copy-start = (bf16[2,384,2048]{2,1,0:T(8,128)(2,1)S(1)}, bf16[2,384,2048]{2,1,0:T(8,128)(2,1)}, u32[]{:S(2)}) copy-start(bf16[2,384,2048]{2,1,0:T(8,128)(2,1)} %param.31) | copy-start | bytes 9437188
  7.2 51.6 %all-gather.19.cloned.1.call-start = ((), (), s32[]{:S(2)}) async-start(), calls=%async_computation.16 | async-start | bytes 1572864 | tf_op jit(solution)/shard_map/all_gather | solution.py:192
  7.9 761.5 %all-gather.9.cloned.1.call-start = ((), (), s32[]{:S(2)}) async-start(), calls=%async_computation.9 | async-start | bytes 1572864 | tf_op jit(solution)/shard_map/all_gather | solution.py:73
  8.7 762.4 %all-gather.13.cloned.1.call-start = ((), (), s32[]{:S(2)}) async-start(), calls=%async_computation.11 | async-start | bytes 1310720 | tf_op jit(solution)/shard_map/all_gather | solution.py:76
  9.4 765.4 %all-gather.11.cloned.1.call-start = ((), (), s32[]{:S(2)}) async-start(), calls=%async_computation.10 | async-start | bytes 1310720 | tf_op jit(solution)/shard_map/all_gather | solution.py:77
  12.8 22.6 copy-start.57
  113.0 800.7 %all-to-all-start.2 = ((bf16[2,16,128,2048]{3,2,0,1:T(8,128)(2,1)}), bf16[2,16,128,2048]{3,2,0,1:T(8,128)(2,1)}, u32[]{:S(2)}, u32[]{:S(2)}) async-start(bf16[2,16,128,2048]{3,2,0,1:T(8,128)(2,1)} %fusion.1), calls=%async_computation.3 | async-start | bytes 33554432 | tf_op jit(solution)/shard_map/all_to_all | solution.py:45
  120.5 411.6 %copy-start.77 = (bf16[512]{0:T(512)(128)(2,1)S(1)}, bf16[512]{0:T(512)(128)(2,1)}, u32[]{:S(2)}) copy-start(bf16[512]{0:T(512)(128)(2,1)} %param.21) | copy-start | bytes 3076
  120.5 657.2 %all-gather.15.cloned.1.call-start = ((), (), s32[]{:S(2)}) async-start(), calls=%async_computation.12 | async-start | bytes 10485760 | tf_op jit(solution)/shard_map/all_gather | solution.py:75
  121.1 671.8 %all-gather.17.cloned.1.call-start = ((), (), s32[]{:S(2)}) async-start(), calls=%async_computation.13 | async-start | bytes 10485760 | tf_op jit(solution)/shard_map/all_gather | solution.py:78
  121.6 740.4 %all-reduce.22.cloned.1.call-start = ((), (), s32[]{:S(2)}) async-start(), calls=%async_computation.14 | async-start | bytes 4194304 | tf_op jit(solution)/shard_map/psum | solution.py:133
  532.1 241.8 %copy-start.64 = (f32[128]{0:T(128)}, f32[128]{0:T(128)S(1)}, u32[]{:S(2)}) copy-start(f32[128]{0:T(128)S(1)} %convert_element_type.248) | copy-start | bytes 1540
  532.1 253.8 %copy-start.68 = (f32[128]{0:T(128)}, f32[128]{0:T(128)S(1)}, u32[]{:S(2)}) copy-start(f32[128]{0:T(128)S(1)} %convert_element_type.251) | copy-start | bytes 1540
  813.0 51.2 %copy-start.48 = (f32[4,1,512]{2,1,0:T(1,128)}, f32[4,1,512]{2,1,0:T(1,128)S(1)}, u32[]{:S(2)}) copy-start(f32[4,1,512]{2,1,0:T(1,128)S(1)} %convert_element_type.315) | copy-start | bytes 24580
  913.7 302.3 %all-to-all-start = ((bf16[2,16,128,2048]{3,2,0,1:T(8,128)(2,1)}), bf16[2,16,128,2048]{3,2,0,1:T(8,128)(2,1)}, u32[]{:S(2)}, u32[]{:S(2)}) async-start(bf16[2,16,128,2048]{3,2,0,1:T(8,128)(2,1)} %copy_select_fusion.1), calls=%async_computation | async-start | bytes 33554432 | tf_op jit(solution)/shard_map/all_to_all | solution.py:45
  1320.6 70.4 %copy-start.52 = (s32[256,8]{0,1:T(8,128)S(1)}, s32[256,8]{0,1:T(8,128)}, u32[]{:S(2)}) copy-start(s32[256,8]{0,1:T(8,128)} %copy-done.51) | copy-start | bytes 24580
  1320.6 367.0 %all-to-all-start.3 = ((bf16[2,16,128,2048]{3,2,0,1:T(8,128)(2,1)}), bf16[2,16,128,2048]{3,2,0,1:T(8,128)(2,1)}, u32[]{:S(2)}, u32[]{:S(2)}) async-start(bf16[2,16,128,2048]{3,2,0,1:T(8,128)(2,1)} %copy.258), calls=%async_computation.4 | async-start | bytes 33554432 | tf_op jit(solution)/shard_map/all_to_all | solution.py:45
  1391.0 534.8 %all-reduce.24.cloned.1.call-start = ((), (), s32[]{:S(2)}) async-start(), calls=%async_computation.17 | async-start | bytes 4194304 | tf_op jit(solution)/shard_map/psum | solution.py:228
  1391.2 401.5 %copy-start.70 = (pred[256]{0:T(512)(128)(4,1)}, pred[256]{0:T(512)(128)(4,1)S(1)}, u32[]{:S(2)}) copy-start(pred[256]{0:T(512)(128)(4,1)S(1)} %get-tuple-element.102) | copy-start | bytes 772
  1391.3 401.5 %copy-start.72 = (pred[256]{0:T(512)(128)(4,1)}, pred[256]{0:T(512)(128)(4,1)S(1)}, u32[]{:S(2)}) copy-start(pred[256]{0:T(512)(128)(4,1)S(1)} %get-tuple-element.103) | copy-start | bytes 772
  1391.3 401.5 %copy-start.74 = (pred[256]{0:T(512)(128)(4,1)}, pred[256]{0:T(512)(128)(4,1)S(1)}, u32[]{:S(2)}) copy-start(pred[256]{0:T(512)(128)(4,1)S(1)} %get-tuple-element.104) | copy-start | bytes 772
  1798.1 127.7 %copy-start.49 = (f32[4,1,512]{2,1,0:T(1,128)S(1)}, f32[4,1,512]{2,1,0:T(1,128)}, u32[]{:S(2)}) copy-start(f32[4,1,512]{2,1,0:T(1,128)} %copy-done.48) | copy-start | bytes 24580
  1798.1 127.7 %copy-start.62 = (f32[256]{0:T(256)S(1)}, f32[256]{0:T(256)}, u32[]{:S(2)}) copy-start(f32[256]{0:T(256)} %copy-done.61) | copy-start | bytes 3076
  1798.1 784.9 %reduce-scatter.12.cloned.1.call-start = ((), (), s32[]{:S(2)}) async-start(), calls=%async_computation.21 | async-start | bytes 1310720 | tf_op jit(solution)/shard_map/reduce_scatter | solution.py:307
  1942.0 641.0 %reduce-scatter.10.cloned.1.call-start = ((), (), s32[]{:S(2)}) async-start(), calls=%async_computation.20 | async-start | bytes 1310720 | tf_op jit(solution)/shard_map/reduce_scatter | solution.py:304
  1951.3 631.7 %reduce-scatter.14.cloned.1.call-start = ((), (), s32[]{:S(2)}) async-start(), calls=%async_computation.22 | async-start | bytes 10485760 | tf_op jit(solution)/shard_map/reduce_scatter | solution.py:310
  1987.5 444.6 %all-to-all-start.1 = ((bf16[2,16,128,2048]{3,2,0,1:T(8,128)(2,1)}), bf16[2,16,128,2048]{3,2,0,1:T(8,128)(2,1)}, u32[]{:S(2)}, u32[]{:S(2)}) async-start(bf16[2,16,128,2048]{3,2,0,1:T(8,128)(2,1)} %copy.252), calls=%async_computation.1 | async-start | bytes 33554432 | tf_op jit(solution)/shard_map/all_to_all | solution.py:45
  1993.4 614.3 %reduce-scatter.8.cloned.1.call-start = ((), (), s32[]{:S(2)}) async-start(), calls=%async_computation.19 | async-start | bytes 10485760 | tf_op jit(solution)/shard_map/reduce_scatter | solution.py:301
  2006.1 749.2 %reduce-scatter.6.cloned.1.call-start = ((), (), s32[]{:S(2)}) async-start(), calls=%async_computation.15 | async-start | bytes 1572864 | tf_op jit(solution)/shard_map/reduce_scatter | solution.py:187
  2543.5 255.6 %all-reduce.26.cloned.1.call-start = ((), (), s32[]{:S(2)}) async-start(), calls=%async_computation.18 | async-start | bytes 2097152 | tf_op jit(solution)/shard_map/psum | solution.py:280
  2567.7 328.0 %all-reduce.28.cloned.1.call-start = ((), (), s32[]{:S(2)}) async-start(), calls=%async_computation.23 | async-start | bytes 9437184 | tf_op jit(solution)/shard_map/psum | solution.py:327
  2757.6 45.7 %copy-start.63 = (bf16[2048]{0:T(1024)(128)(2,1)S(1)}, bf16[2048]{0:T(1024)(128)(2,1)}, u32[]{:S(2)}) copy-start(bf16[2048]{0:T(1024)(128)(2,1)} %get-tuple-element.14) | copy-start | bytes 12292
  (68 other events, 272.3 us)
Sparse Core Ops, SparseCore 0:
  9.5 23.9 all-gather.18
  35.1 21.2 all-gather.8
  58.0 27.9 all-gather.12
  87.5 27.3 all-gather.10
  122.5 385.1 all-gather.14
  509.2 228.2 all-gather.16
  800.4 61.5 all-reduce.21
  1798.2 127.5 all-reduce.23
  1942.2 27.2 reduce-scatter.11
  1971.6 25.7 reduce-scatter.9
  1999.8 367.0 reduce-scatter.13
  2369.1 238.4 reduce-scatter.7
  2610.4 144.7 reduce-scatter.5
  2758.0 40.9 all-reduce.25
  2801.5 94.1 all-reduce.27
where the time goes:
time: 2920 us; the launch traced here: 2910 us
  waiting for transfers between devices  1440 us (49%)
  blocking collectives  680 us (23%)
  local copies, waits for them, and re-layouts  397 us (14%)
  matrix products  201 us (7%)
  starting transfers between devices  89.9 us (3%)
  other arithmetic  84.7 us (3%)
    all_to_all x4, waiting for transfers between devices, route_rows(): lax.all_to_all(buffer, ('dp', 'expert'), split_axis=1, concat_axis=1, til...  1000 us
    unnamed x2, blocking collectives  421 us
    all_gather x1, blocking collectives, local(): lax.all_gather(attention_gain, 'dp', axis=0, tiled=True)  236 us
    reduce_scatter x1, waiting for transfers between devices, local(): lax.psum_scatter(combined.astype(jnp.bfloat16), 'tensor', scatter_dimensi...  135 us
    psum x1, waiting for transfers between devices, local(): expert_in_grad = lax.psum(expert_in_part, 'tensor')  123 us
    gather x8, local copies, waits for them, and re-layouts, local(): jnp.take(returned, slot_index[:, slot_rank], axis=0).astype(jnp.float32)  91.4 us
    gather x8, local copies, waits for them, and re-layouts, local(): jnp.take(returned_back, slot_index[:, slot_rank], axis=0)  90.6 us
    all_to_all x4, starting transfers between devices, route_rows(): lax.all_to_all(buffer, ('dp', 'expert'), split_axis=1, concat_axis=1, til...  89.3 us
  transfers between devices with their start and end apart: 19, of which 9 were waited for; matrix products, arithmetic and copies ran while one was open for 15% of the time, Pallas kernels for 0%

commit v1 on v0

v1 whole, which is shorter than its diff:
```python
import math

import jax
import jax.numpy as jnp
from jax import lax
from jax.sharding import PartitionSpec as P

HEAD_SIZE = 128
SEQ = 256
CHUNK_TOKENS = 4096
ROWS = ("dp", "expert")
WHOLE = ("tensor", "dp", "expert")

epsilon = 1e-06
rope_base = 1000000.0


def rope_tables(positions):
    half_dim = HEAD_SIZE // 2
    frequency = rope_base ** (-(jnp.arange(half_dim, dtype=jnp.float32) * 2.0) / HEAD_SIZE)
    angles = positions.astype(jnp.float32)[:, None] * frequency[None, :]
    angles = jnp.concatenate([angles, angles], axis=1)
    return (jnp.cos(angles)[:, None, :], jnp.sin(angles)[:, None, :])


def prepare(values, scales, cosine, sine_table, factor):
    mean_sq = jnp.mean(values * values, axis=-1, keepdims=True)
    normed = values * lax.rsqrt(mean_sq + epsilon) * scales
    half_dim = values.shape[-1] // 2
    turned = jnp.concatenate([-normed[..., half_dim:], normed[..., :half_dim]], axis=-1)
    return (normed * cosine + turned * sine_table) * factor


def dot(first_arr, second_arr):
    return jnp.dot(first_arr, second_arr, preferred_element_type=jnp.float32)


def dot_last(first_arr, second_arr):
    return lax.dot_general(
        first_arr, second_arr, (((1,), (1,)), ((), ())), preferred_element_type=jnp.float32
    )


def dot_first(first_arr, second_arr):
    return lax.dot_general(
        first_arr, second_arr, (((0,), (0,)), ((), ())), preferred_element_type=jnp.float32
    )


def own_rows(weight):
    rows = weight.shape[0] // lax.axis_size("expert")
    return lax.dynamic_slice_in_dim(weight, lax.axis_index("expert") * rows, rows, 0)


def gather_weight(weight):
    return lax.all_gather(weight, ROWS, axis=0, tiled=True)


def scatter_weight(gradient):
    piece = lax.psum_scatter(gradient.astype(jnp.bfloat16), ROWS, scatter_dimension=0, tiled=True)
    return lax.all_gather(piece, "expert", axis=0, tiled=True).astype(jnp.float32)


def local(
    block_in,
    route_ids,
    route_weights,
    cotangent,
    attention_gain,
    query_weight,
    key_projection_matrix,
    value_projection_matrix,
    output_weight,
    query_gain,
    key_gain,
    expert_gain,
    expert_gate_matrix,
    expert_up_matrix,
    expert_down_matrix,
):
    row_count, half_width = block_in.shape
    halves = lax.axis_size("tensor")
    model_width = half_width * halves
    group_devices = lax.axis_size(ROWS)
    local_experts = expert_gate_matrix.shape[0]
    expert_total = local_experts * group_devices
    hidden = expert_gate_matrix.shape[2]
    offset = lax.axis_index("tensor") * half_width
    group_index = lax.axis_index(ROWS)

    expert_names = jnp.arange(expert_total, dtype=jnp.int32)
    dense = jnp.sum(
        jnp.where(
            route_ids[:, :, None] == expert_names[None, None, :], route_weights[:, :, None], 0.0
        ),
        axis=1,
    ).T
    gains = jnp.concatenate([attention_gain, expert_gain, query_gain, key_gain]).astype(jnp.float32)
    table = jnp.concatenate([dense.reshape(-1), gains])
    table = lax.all_gather(table, ROWS, axis=0, tiled=False)
    full_in = lax.all_gather(block_in, "tensor", axis=1, tiled=True)

    qkv_full = gather_weight(
        jnp.concatenate(
            [
                own_rows(query_weight),
                own_rows(key_projection_matrix),
                own_rows(value_projection_matrix),
            ],
            axis=1,
        )
    )
    output_full = gather_weight(own_rows(output_weight))

    routed = table[:, : expert_total * row_count].reshape(group_devices, expert_total, row_count)
    routed = lax.dynamic_slice_in_dim(routed, group_index * local_experts, local_experts, 1)
    gain_rows = table[:, expert_total * row_count :].reshape(
        lax.axis_size("dp"), lax.axis_size("expert"), -1
    )[:, 0]
    width_rows = attention_gain.shape[0]
    head_rows = query_gain.shape[0]
    norm_first = gain_rows[:, :width_rows].reshape(-1)
    norm_second = gain_rows[:, width_rows : 2 * width_rows].reshape(-1)
    query_scale = gain_rows[:, 2 * width_rows : 2 * width_rows + head_rows].reshape(-1)
    key_scale = gain_rows[:, 2 * width_rows + head_rows :].reshape(-1)
    first_half = lax.dynamic_slice_in_dim(norm_first, offset, half_width, 0)
    second_half = lax.dynamic_slice_in_dim(norm_second, offset, half_width, 0)

    input_float = full_in.astype(jnp.float32)
    inv_first = lax.rsqrt(jnp.mean(input_float * input_float, axis=1, keepdims=True) + epsilon)
    normed = (input_float * inv_first * norm_first).astype(jnp.bfloat16)
    block_float = block_in.astype(jnp.float32)
    input_hat = block_float * inv_first
    query_cols = query_weight.shape[1]
    key_cols = key_projection_matrix.shape[1]
    heads_local = query_cols // HEAD_SIZE
    key_heads = key_cols // HEAD_SIZE
    group_size = heads_local // key_heads
    seq_count = row_count // SEQ
    projected = dot(normed, qkv_full)
    queries = projected[:, :query_cols].reshape(row_count, heads_local, HEAD_SIZE)
    key_rows = projected[:, query_cols : query_cols + key_cols].reshape(
        row_count, key_heads, HEAD_SIZE
    )
    value_rows = projected[:, query_cols + key_cols :].astype(jnp.bfloat16)
    positions = jnp.arange(row_count, dtype=jnp.int32) % SEQ
    cosine, sine_table = rope_tables(positions)
    factor = 1.0 / math.sqrt(HEAD_SIZE)
    query_rot = prepare(queries, query_scale, cosine, sine_table, factor).astype(jnp.bfloat16)
    key_rot = prepare(key_rows, key_scale, cosine, sine_table, 1.0).astype(jnp.bfloat16)
    query_seq = query_rot.reshape(seq_count, SEQ, key_heads, group_size, HEAD_SIZE)
    key_seq = key_rot.reshape(seq_count, SEQ, key_heads, HEAD_SIZE)
    value_seq = value_rows.reshape(seq_count, SEQ, key_heads, HEAD_SIZE)
    causal = jnp.arange(SEQ)[None, :] <= jnp.arange(SEQ)[:, None]
    scores = jnp.einsum("nqhgd,nkhd->nhgqk", query_seq, key_seq, preferred_element_type=jnp.float32)
    log_total = jnp.log(jnp.sum(jnp.where(causal, jnp.exp(scores), 0.0), axis=-1))
    soft_weights = jnp.where(causal, jnp.exp(scores - log_total[..., None]), 0.0)
    prob_half = soft_weights.astype(jnp.bfloat16)
    attended = (
        jnp.einsum("nhgqk,nkhd->nqhgd", prob_half, value_seq, preferred_element_type=jnp.float32)
        .astype(jnp.bfloat16)
        .reshape(row_count, heads_local * HEAD_SIZE)
    )
    head_total = lax.psum_scatter(
        dot_last(attended, output_full), "tensor", scatter_dimension=1, tiled=True
    )
    residual = block_float + head_total
    square_sum = lax.psum(jnp.sum(residual * residual, axis=1), "tensor")[:, None]
    inv_second = lax.rsqrt(square_sum / model_width + epsilon)
    resid_hat = residual * inv_second
    expert_in = (resid_hat * second_half).astype(jnp.bfloat16)

    first_layer = jnp.concatenate(
        [expert_gate_matrix[index] for index in range(local_experts)]
        + [expert_up_matrix[index] for index in range(local_experts)],
        axis=1,
    ).reshape(halves, half_width, 2 * local_experts * hidden)
    down = expert_down_matrix.reshape(local_experts * hidden, halves, half_width)
    down_halves = [down[:, index] for index in range(halves)]
    hidden_all = local_experts * hidden

    chunk_count = max(1, group_devices * row_count // CHUNK_TOKENS)
    chunk_rows = row_count // chunk_count
    chunk_total = chunk_rows * group_devices

    def everywhere(rows):
        gathered = lax.all_gather(rows, WHOLE, axis=0, tiled=True)
        return gathered.reshape(halves, chunk_total, half_width)

    mixture_parts, expert_back_parts = [], []
    down_grad = gate_grad = up_matrix_gradient = 0.0
    for chunk in range(chunk_count):
        low = chunk * chunk_rows
        rows_in = everywhere(expert_in[low : low + chunk_rows])
        rows_cot = everywhere(cotangent[low : low + chunk_rows])
        weight_cols = jnp.repeat(
            routed[:, :, low : low + chunk_rows]
            .transpose(0, 2, 1)
            .reshape(chunk_total, local_experts),
            hidden,
            axis=1,
        )
        hidden_pre = sum(dot(rows_in[index], first_layer[index]) for index in range(halves))
        gate_pre = hidden_pre[:, :hidden_all]
        up_pre = hidden_pre[:, hidden_all:]
        sigmoid = jax.nn.sigmoid(gate_pre)
        swish = gate_pre * sigmoid
        weighted = (swish * up_pre * weight_cols).astype(jnp.bfloat16)
        mixed = jnp.stack([dot(weighted, piece) for piece in down_halves])
        mixture_parts.append(
            lax.psum_scatter(
                mixed.astype(jnp.bfloat16).reshape(halves * chunk_total, half_width),
                WHOLE,
                scatter_dimension=0,
                tiled=True,
            )
        )
        act_grad = weight_cols * sum(
            dot_last(rows_cot[index], down_halves[index]) for index in range(halves)
        )
        gate_back = (act_grad * up_pre * sigmoid * (1.0 + gate_pre * (1.0 - sigmoid))).astype(
            jnp.bfloat16
        )
        up_back = (act_grad * swish).astype(jnp.bfloat16)
        both_back = jnp.concatenate([gate_back, up_back], axis=1)
        back = jnp.stack([dot_last(both_back, first_layer[index]) for index in range(halves)])
        expert_back_parts.append(
            lax.psum_scatter(
                back.astype(jnp.bfloat16).reshape(halves * chunk_total, half_width),
                WHOLE,
                scatter_dimension=0,
                tiled=True,
            )
        )
        down_grad = down_grad + jnp.concatenate(
            [dot_first(weighted, rows_cot[index]) for index in range(halves)], axis=1
        ).reshape(local_experts, hidden, model_width)
        gate_grad = gate_grad + jnp.stack(
            [
                jnp.concatenate(
                    [
                        dot_first(rows_in[index], gate_back[:, e * hidden : (e + 1) * hidden])
                        for index in range(halves)
                    ]
                )
                for e in range(local_experts)
            ]
        )
        up_matrix_gradient = up_matrix_gradient + jnp.stack(
            [
                jnp.concatenate(
                    [
                        dot_first(rows_in[index], up_back[:, e * hidden : (e + 1) * hidden])
                        for index in range(halves)
                    ]
                )
                for e in range(local_experts)
            ]
        )
    mixture = jnp.concatenate(mixture_parts).astype(jnp.float32)
    block_out = (residual + mixture).astype(jnp.bfloat16)
    expert_in_grad = jnp.concatenate(expert_back_parts).astype(jnp.float32)

    grad_float = cotangent.astype(jnp.float32)
    scaled = expert_in_grad * second_half
    back_mean = lax.psum(jnp.sum(scaled * resid_hat, axis=1), "tensor")[:, None] / model_width
    resid_grad = grad_float + inv_second * (scaled - resid_hat * back_mean)
    expert_gain_part = jnp.sum(expert_in_grad * resid_hat, axis=0)
    resid_cast = lax.all_gather(resid_grad.astype(jnp.bfloat16), "tensor", axis=1, tiled=True)
    output_weight_grad = scatter_weight(dot_first(resid_cast, attended))
    attended_grad = dot(resid_cast, output_full).astype(jnp.bfloat16)
    scores_again = jnp.einsum(
        "nqhgd,nkhd->nhgqk", query_seq, key_seq, preferred_element_type=jnp.float32
    )
    probs_again = jnp.where(causal, jnp.exp(scores_again - log_total[..., None]), 0.0)
    probs_again_half = probs_again.astype(jnp.bfloat16)
    grad_seq = attended_grad.reshape(seq_count, SEQ, key_heads, group_size, HEAD_SIZE)
    value_grad = (
        jnp.einsum(
            "nhgqk,nqhgd->nkhd", probs_again_half, grad_seq, preferred_element_type=jnp.float32
        )
        .astype(jnp.bfloat16)
        .reshape(row_count, key_heads * HEAD_SIZE)
    )
    prob_grad = jnp.einsum(
        "nqhgd,nkhd->nhgqk", grad_seq, value_seq, preferred_element_type=jnp.float32
    )
    row_inner = jnp.sum(probs_again * prob_grad, axis=-1, keepdims=True)
    score_grad = (probs_again * (prob_grad - row_inner)).astype(jnp.bfloat16)
    query_rot_grad = jnp.einsum(
        "nhgqk,nkhd->nqhgd", score_grad, key_seq, preferred_element_type=jnp.float32
    ).reshape(row_count, heads_local, HEAD_SIZE)
    key_rot_grad = jnp.einsum(
        "nhgqk,nqhgd->nkhd", score_grad, query_seq, preferred_element_type=jnp.float32
    ).reshape(row_count, key_heads, HEAD_SIZE)
    _, query_pull = jax.vjp(
        lambda values, scales: prepare(values, scales, cosine, sine_table, factor),
        queries,
        query_scale,
    )
    query_grad, query_scale_grad = query_pull(query_rot_grad)
    _, key_pull = jax.vjp(
        lambda values, scales: prepare(values, scales, cosine, sine_table, 1.0), key_rows, key_scale
    )
    key_grad, key_scale_grad = key_pull(key_rot_grad)
    casts = jnp.concatenate(
        [
            query_grad.reshape(row_count, query_cols).astype(jnp.bfloat16),
            key_grad.reshape(row_count, key_cols).astype(jnp.bfloat16),
            value_grad,
        ],
        axis=1,
    )
    normed_grad = lax.psum_scatter(
        dot_last(casts, qkv_full).astype(jnp.bfloat16), "tensor", scatter_dimension=1, tiled=True
    ).astype(jnp.float32)
    qkv_grad = scatter_weight(dot_first(normed, casts))
    scaled_first = normed_grad * first_half
    first_mean = lax.psum(jnp.sum(scaled_first * input_hat, axis=1), "tensor")[:, None]
    block_in_grad = resid_grad + inv_first * (scaled_first - input_hat * first_mean / model_width)
    attention_gain_part = jnp.sum(normed_grad * input_hat, axis=0)

    wide = jnp.zeros((2, model_width), jnp.float32)
    wide = lax.dynamic_update_slice(
        wide, jnp.stack([attention_gain_part, expert_gain_part]), (0, offset)
    )
    small = jnp.concatenate([wide[0], wide[1], query_scale_grad, key_scale_grad])
    small = lax.psum(small, WHOLE)
    dp_index = lax.axis_index("dp")

    def owned(start, rows):
        return lax.dynamic_slice_in_dim(small, start + dp_index * rows, rows, 0)

    return (
        block_out,
        block_in_grad,
        owned(0, width_rows),
        qkv_grad[:, :query_cols],
        qkv_grad[:, query_cols : query_cols + key_cols],
        qkv_grad[:, query_cols + key_cols :],
        output_weight_grad,
        owned(2 * model_width, head_rows),
        owned(2 * model_width + HEAD_SIZE, head_rows),
        owned(model_width, width_rows),
        gate_grad,
        up_matrix_gradient,
        down_grad,
    )


def solution(mesh):
    rows = P(ROWS, "tensor")
    weight = P("dp", "tensor")
    expert_cols = P(ROWS, None, "tensor")
    expert_rows = P(ROWS, "tensor", None)
    gain = P("dp")
    placed = (rows, P(ROWS, None), P(ROWS, None), rows, gain) + (weight,) * 4 + (gain,) * 3
    return jax.shard_map(
        local,
        mesh=mesh,
        in_specs=placed + (expert_cols, expert_cols, expert_rows),
        out_specs=(rows, rows, gain)
        + (weight,) * 4
        + (gain,) * 3
        + (expert_cols, expert_cols, expert_rows),
        check_vma=False,
    )
```

time: 2920 us -> 1280 us (0.44)
  waiting for transfers between devices: 1440 us -> 776 us
  blocking collectives: 680 us -> 60.8 us
  local copies, waits for them, and re-layouts: 397 us -> 49.6 us
  matrix products: 201 us -> 291 us
  starting transfers between devices: 89.9 us -> 0.98 us
    all_to_all x4 -> x0, waiting for transfers between devices: 1000 us -> none  [route_rows(): lax.all_to_all(buffer, ('dp', 'expert'), split_axis=1, concat_axis=1, til...]
    unnamed x2 -> x0, blocking collectives: 421 us -> none
    gather x24 -> x0, local copies, waits for them, and re-layouts: 285 us -> none  [the longest x8 91.4 us: local(): jnp.take(returned, slot_index[:, slot_rank], axis=0).astype(jnp.float32)]
    psum x4 -> x0, waiting for transfers between devices: 276 us -> none  [the longest x1 123 us: local(): expert_in_grad = lax.psum(expert_in_part, 'tensor')]
    reduce_scatter x5 -> x6, waiting for transfers between devices: 159 us -> 418 us  [the longest x1 182 us: local(): lax.psum_scatter(back.astype(jnp.bfloat16).reshape(halves * chunk_total,...]
    all_gather x2 -> x0, blocking collectives: 248 us -> none  [the longest x1 236 us: local(): lax.all_gather(attention_gain, 'dp', axis=0, tiled=True)]
    all_gather x5 -> x7, waiting for transfers between devices: 0.05 us -> 223 us  [the longest x2 175 us: everywhere(): gathered = lax.all_gather(rows, WHOLE, axis=0, tiled=True)]
    unnamed x15 -> x16, waiting for transfers between devices: 3.78 us -> 135 us
  transfers between devices with their start and end apart: 19 -> 15, of which waited for: 9 -> 10; matrix products, arithmetic and copies ran while one was open for 15% -> 19% of each run, Pallas kernels for 0% -> 0%
where the time goes in v1:
time: 1280 us; the launch traced here: 1270 us
  waiting for transfers between devices  776 us (61%)
  matrix products  291 us (23%)
  other arithmetic  74.9 us (6%)
  blocking collectives  60.8 us (5%)
  local copies, waits for them, and re-layouts  49.6 us (4%)
  between operations  17.9 us (1%)
    reduce_scatter x1, waiting for transfers between devices, local(): lax.psum_scatter(back.astype(jnp.bfloat16).reshape(halves * chunk_total,...  182 us
    all_gather x2, waiting for transfers between devices, everywhere(): gathered = lax.all_gather(rows, WHOLE, axis=0, tiled=True)  175 us
    unnamed x16, waiting for transfers between devices  135 us
    reduce_scatter x1, waiting for transfers between devices, local(): lax.psum_scatter(mixed.astype(jnp.bfloat16).reshape(halves * chunk_total,...  133 us
    dot_general x12, matrix products, dot_first(): lax.dot_general(first_arr, second_arr, (((0,), (0,)), ((), ())), preferre...  102 us
    dot_general x6, matrix products, dot_last(): lax.dot_general(first_arr, second_arr, (((1,), (1,)), ((), ())), preferre...  95.9 us
    dot_general x6, matrix products, dot(): return jnp.dot(first_arr, second_arr, preferred_element_type=jnp.float32)  85.1 us
    reduce_scatter x2, waiting for transfers between devices, scatter_weight(): lax.psum_scatter(gradient.astype(jnp.bfloat16), ROWS, scatter_dimension=0...  70 us
  transfers between devices with their start and end apart: 15, of which 10 were waited for; matrix products, arithmetic and copies ran while one was open for 19% of the time, Pallas kernels for 0%

profile of v1, /device:TPU:0, one launch (start us, length us, event | category | flops | bytes accessed | tf_op | source)
XLA Modules:
  0.0 1271.5 jit_solution(16060481617325919106)
XLA Ops:
  20.7 134.0 %all-reduce.7.cloned.1.call-done = f32[148480]{0:T(1024)} async-done(((f32[148480]{0:T(1024)}), f32[148480]{0:T(1024)}) %all-reduce.7.cloned.1.call-update) | async-done | bytes 593936
  183.0 24.3 %all-gather.14.cloned.1.call-done = bf16[2048,2048]{1,0:T(8,128)(2,1)} async-done(((bf16[128,2048]{1,0:T(8,128)(2,1)}), bf16[2048,2048]{1,0:T(8,128)(2,1)}) %all-gather.14.cloned.1.call-update) | async-done | bytes 8388624 | tf_op jit(solution)/shard_map/all_gather | solution.py:56
  207.3 7.5 fusion.119
  215.6 30.1 %reduce-scatter.7.cloned.1.call-done = f32[256,1024]{1,0:T(8,128)} async-done(((f32[256,2048]{1,0:T(8,128)}), f32[256,1024]{1,0:T(8,128)}) %reduce-scatter.7.cloned.1.call-update) | async-done | bytes 1048592 | tf_op jit(solution)/shard_map/reduce_scatter | solution.py:164
  273.2 73.0 %all-gather.18.cloned.1.call-done = bf16[8192,1024]{1,0:T(8,128)(2,1)} async-done(((bf16[256,1024]{1,0:T(8,128)(2,1)}), bf16[8192,1024]{1,0:T(8,128)(2,1)}) %all-gather.18.cloned.1.call-update) | async-done | bytes 16777232 | tf_op jit(solution)/shard_map/all_gather | solution.py:187
  346.3 13.8 %fusion.6 = f32[4096,768]{0,1:T(8,128)} fusion(bf16[8192,1024]{1,0:T(8,128)(2,1)} %all-gather.18.cloned.1.call-done, bf16[768,1,1024]{2,1,0:T(2,128)(2,1)} %get-tuple-element.29), kind=kOutput, calls=%fused_computation.21 | convolution fusion | flops 6442450944 | bytes 24117248 | tf_op jit(solution)/shard_map/dot_general | solution.py:39
  360.1 102.3 %all-gather.16.cloned.1.call-done = bf16[8192,1024]{1,0:T(8,128)(2,1)} async-done(((bf16[256,1024]{1,0:T(8,128)(2,1)}), bf16[8192,1024]{1,0:T(8,128)(2,1)}) %all-gather.16.cloned.1.call-update) | async-done | bytes 16777232 | tf_op jit(solution)/shard_map/all_gather | solution.py:187
  462.4 21.1 %fusion.31 = f32[4096,1536]{0,1:T(8,128)} fusion(bf16[8192,1024]{1,0:T(8,128)(2,1)} %all-gather.16.cloned.1.call-done, bf16[2048,1536]{1,0:T(8,128)(2,1)} %pad_maximum_fusion.9), kind=kOutput, calls=%fused_computation.48 | convolution fusion | flops 12884901888 | bytes 36700160 | tf_op jit(solution)/shard_map/dot_general | solution.py:35
  483.4 28.2 %convolution_add_fusion = f32[4096,1536]{0,1:T(8,128)} fusion(f32[4096,1536]{0,1:T(8,128)} %fusion.31, bf16[8192,1024]{1,0:T(8,128)(2,1)} %all-gather.16.cloned.1.call-done, bf16[2048,1536]{1,0:T(8,128)(2,1)} %pad_maximum_fusion.9), kind=kOutput, calls=%fused_computation.2 | convolution fusion | flops 12891193344 | bytes 61865984 | tf_op jit(solution)/shard_map/dot_general | solution.py:35
  511.6 27.8 %multiply_convert_fusion.1 = (bf16[4096,768]{0,1:T(8,128)(2,1)}, bf16[4096,768]{0,1:T(8,128)(2,1)}, bf16[4096,768]{0,1:T(8,128)(2,1)}) fusion(f32[4096,1536]{0,1:T(8,128)} %convolution_add_fusion, f32[4096,2]{0,1:T(2,128)S(1)} %bitcast.216, f32[4096,768]{0,1:T(8,128)} %fusion.6, bf16[768,1,1024]{2,1,0:T(2,128)(2,1)} %get-tuple-element.28, ...), kind=kOutput, calls=%fused_computation.8 | convolution fusion | flops 6499074048 | bytes 68190208 | tf_op jit(solution)/shard_map/dot_general | solution.py:39
  539.5 19.3 %convert_bitcast_fusion.1 = bf16[1,4096,1024]{2,1,0:T(8,128)(2,1)} fusion(bf16[4096,768]{0,1:T(8,128)(2,1)} %get-tuple-element.26, bf16[4096,768]{0,1:T(8,128)(2,1)} %get-tuple-element.25, bf16[2048,1536]{1,0:T(8,128)(2,1)} %pad_maximum_fusion.9), kind=kOutput, calls=%fused_computation.13 | convolution fusion | flops 12914262016 | bytes 24117248 | tf_op jit(solution)/shard_map/dot_general | solution.py:39
  558.8 19.6 %convert_bitcast_fusion = bf16[1,4096,1024]{2,1,0:T(8,128)(2,1)} fusion(bf16[4096,768]{0,1:T(8,128)(2,1)} %get-tuple-element.26, bf16[4096,768]{0,1:T(8,128)(2,1)} %get-tuple-element.25, bf16[2048,1536]{1,0:T(8,128)(2,1)} %pad_maximum_fusion.9), kind=kOutput, calls=%fused_computation.12 | convolution fusion | flops 12914262016 | bytes 24117248 | tf_op jit(solution)/shard_map/dot_general | solution.py:39
  578.4 13.8 %pad_maximum_fusion.1 = bf16[2,4096,1024]{2,1,0:T(8,128)(2,1)} fusion(bf16[1,4096,1024]{2,1,0:T(8,128)(2,1)} %convert_bitcast_fusion, bf16[1,4096,1024]{2,1,0:T(8,128)(2,1)} %convert_bitcast_fusion.1), kind=kLoop, calls=%fused_computation.4 | loop fusion | flops 8388608 | bytes 33554432 | tf_op jit(solution)/shard_map/stack | solution.py:226
  592.3 181.6 %reduce-scatter.11.cloned.1.call-done = bf16[256,1024]{1,0:T(8,128)(2,1)} async-done(((bf16[8192,1024]{1,0:T(8,128)(2,1)}), bf16[256,1024]{1,0:T(8,128)(2,1)}) %reduce-scatter.11.cloned.1.call-update) | async-done | bytes 524304 | tf_op jit(solution)/shard_map/reduce_scatter | solution.py:228
  783.1 22.9 %all-gather.20.cloned.1.call-done = bf16[256,2048]{1,0:T(8,128)(2,1)} async-done(((bf16[256,1024]{1,0:T(8,128)(2,1)}), bf16[256,2048]{1,0:T(8,128)(2,1)}) %all-gather.20.cloned.1.call-update) | async-done | bytes 1048592 | tf_op jit(solution)/shard_map/all_gather | solution.py:269
  841.4 12.9 %convert_bitcast_fusion.2 = bf16[1,4096,1024]{2,1,0:T(8,128)(2,1)} fusion(bf16[4096,768]{0,1:T(8,128)(2,1)} %get-tuple-element.27, bf16[768,1,1024]{2,1,0:T(2,128)(2,1)} %get-tuple-element.29), kind=kOutput, calls=%fused_computation.14 | convolution fusion | flops 6446645248 | bytes 16252928 | tf_op jit(solution)/shard_map/dot_general | solution.py:35
  854.3 7.9 convolution_convert_fusion.2
  862.3 10.6 convert_bitcast_fusion.3
  872.8 10.6 pad_maximum_fusion
  883.6 9.2 fusion.16
  892.7 8.1 fusion.25
  901.1 7.0 fusion.14
  908.1 7.1 fusion.23
  920.4 8.1 fusion.20
  928.6 9.0 fusion.29
  937.6 7.5 fusion.18
  949.1 11.1 fusion.27
  960.3 10.4 fusion.4
  970.7 70.0 %reduce-scatter.15.cloned.1.call-done = bf16[128,2560]{1,0:T(8,128)(2,1)} async-done(((bf16[2048,2560]{1,0:T(8,128)(2,1)}), bf16[128,2560]{1,0:T(8,128)(2,1)}) %reduce-scatter.15.cloned.1.call-update) | async-done | bytes 655376 | tf_op jit(solution)/shard_map/reduce_scatter | solution.py:60
  1042.3 11.1 fusion.8
  1069.8 46.1 %psum.31 = f32[4352]{0:T(1024)S(1)} all-reduce(f32[4352]{0:T(1024)S(1)} %pad_maximum_fusion.18), channel_id=1, replica_groups=mesh['dp'=4,'tensor'=2,'expert'=4] {'tensor','dp','expert'}, use_global_device_ids=true, to_apply=%region_22.23 | all-reduce | flops 4352 | bytes 34816 | tf_op jit(solution)/shard_map/psum | solution.py:328
  1117.1 133.0 %reduce-scatter.9.cloned.1.call-done = bf16[256,1024]{1,0:T(8,128)(2,1)} async-done(((bf16[8192,1024]{1,0:T(8,128)(2,1)}), bf16[256,1024]{1,0:T(8,128)(2,1)}) %reduce-scatter.9.cloned.1.call-update) | async-done | bytes 524304 | tf_op jit(solution)/shard_map/reduce_scatter | solution.py:211
  (301 shorter events, 154.6 us)
Async XLA Ops:
  8.0 146.7 %all-reduce.7.cloned.1.call-start = ((), (), s32[]{:S(2)}) async-start(), calls=%async_computation.20 | async-start | bytes 1187840
  14.8 141.5 %all-gather.10.cloned.1.call-start = ((), (), s32[]{:S(2)}) async-start(), calls=%async_computation.6 | async-start | bytes 1572864 | tf_op jit(solution)/shard_map/all_gather | solution.py:101
  15.4 142.5 %all-gather.12.cloned.1.call-start = ((), (), s32[]{:S(2)}) async-start(), calls=%async_computation.7 | async-start | bytes 11141120 | tf_op jit(solution)/shard_map/all_gather | solution.py:56
  17.3 189.9 %all-gather.14.cloned.1.call-start = ((), (), s32[]{:S(2)}) async-start(), calls=%async_computation.8 | async-start | bytes 8912896 | tf_op jit(solution)/shard_map/all_gather | solution.py:56
  19.3 226.4 %reduce-scatter.7.cloned.1.call-start = ((), (), s32[]{:S(2)}) async-start(), calls=%async_computation.9 | async-start | bytes 3145728 | tf_op jit(solution)/shard_map/reduce_scatter | solution.py:164
  19.4 158.9 %copy-start.26 = (pred[256,256]{0,1:T(8,128)(4,1)}, pred[256,256]{0,1:T(8,128)(4,1)S(1)}, u32[]{:S(2)}) copy-start(pred[256,256]{0,1:T(8,128)(4,1)S(1)} %iota_compare_fusion) | copy-start | bytes 196612
  20.7 152.7 %copy-start.24 = (f32[256,128]{0,1:T(8,128)}, f32[256,128]{0,1:T(8,128)S(1)}, u32[]{:S(2)}) copy-start(f32[256,128]{0,1:T(8,128)S(1)} %get-tuple-element.48) | copy-start | bytes 393220
  181.3 33.4 %copy-start.9 = (bf16[2,8,256,256]{2,3,1,0:T(8,128)(2,1)}, bf16[2,8,256,256]{2,3,1,0:T(8,128)(2,1)S(1)}, u32[]{:S(2)}) copy-start(bf16[2,8,256,256]{2,3,1,0:T(8,128)(2,1)S(1)} %fusion.56) | copy-start | bytes 6291460
  207.3 38.5 %copy-start.14 = (bf16[256,1024]{1,0:T(8,128)(2,1)S(1)}, bf16[256,1024]{1,0:T(8,128)(2,1)}, u32[]{:S(2)}) copy-start(bf16[256,1024]{1,0:T(8,128)(2,1)} %param.15) | copy-start | bytes 1572868
  214.8 131.5 %all-gather.18.cloned.1.call-start = ((), (), s32[]{:S(2)}) async-start(), calls=%async_computation.12 | async-start | bytes 17301504 | tf_op jit(solution)/shard_map/all_gather | solution.py:187
  215.5 246.8 %all-gather.16.cloned.1.call-start = ((), (), s32[]{:S(2)}) async-start(), calls=%async_computation.10 | async-start | bytes 17301504 | tf_op jit(solution)/shard_map/all_gather | solution.py:187
  215.6 44.1 %copy-start.49 = (f32[1024]{0:T(1024)}, f32[1024]{0:T(1024)S(1)}, u32[]{:S(2)}) copy-start(f32[1024]{0:T(1024)S(1)} %dynamic_slice.37) | copy-start | bytes 12292
  253.1 520.8 %reduce-scatter.11.cloned.1.call-start = ((), (), s32[]{:S(2)}) async-start(), calls=%async_computation.13 | async-start | bytes 17301504 | tf_op jit(solution)/shard_map/reduce_scatter | solution.py:228
  592.2 181.7 %copy-start.7 = (f32[256,1024]{1,0:T(8,128)S(1)}, f32[256,1024]{1,0:T(8,128)}, u32[]{:S(2)}) copy-start(f32[256,1024]{1,0:T(8,128)} %copy-done.6) | copy-start | bytes 3145732
  592.2 181.7 %copy-start.50 = (f32[1024]{0:T(1024)S(1)}, f32[1024]{0:T(1024)}, u32[]{:S(2)}) copy-start(f32[1024]{0:T(1024)} %copy-done.49) | copy-start | bytes 12292
  592.2 181.7 %copy-start.58 = (f32[256]{0:T(256)S(1)}, f32[256]{0:T(256)}, u32[]{:S(2)}) copy-start(f32[256]{0:T(256)} %copy-done.57) | copy-start | bytes 3076
  592.2 188.7 %copy-start.20 = (bf16[256,1024]{1,0:T(8,128)(2,1)S(1)}, bf16[256,1024]{1,0:T(8,128)(2,1)}, u32[]{:S(2)}) copy-start(bf16[256,1024]{1,0:T(8,128)(2,1)} %param.18) | copy-start | bytes 1572868
  592.2 213.8 %copy-start.23 = (bf16[2,128,8,256]{3,1,2,0:T(8,128)(2,1)S(1)}, bf16[2,128,8,256]{3,1,2,0:T(8,128)(2,1)}, u32[]{:S(2)}) copy-start(bf16[2,128,8,256]{3,1,2,0:T(8,128)(2,1)} %convolution_convert_fusion.4) | copy-start | bytes 3145732
  592.2 213.8 %all-gather.20.cloned.1.call-start = ((), (), s32[]{:S(2)}) async-start(), calls=%async_computation.14 | async-start | bytes 1572864 | tf_op jit(solution)/shard_map/all_gather | solution.py:269
  780.9 32.1 %copy-start.67 = (f32[256]{0:T(256)}, f32[256]{0:T(256)S(1)}, u32[]{:S(2)}) copy-start(f32[256]{0:T(256)S(1)} %broadcast_multiply_fusion.4) | copy-start | bytes 3076
  783.1 162.1 %reduce-scatter.17.cloned.1.call-start = ((), (), s32[]{:S(2)}) async-start(), calls=%async_computation.18 | async-start | bytes 8912896 | tf_op jit(solution)/shard_map/reduce_scatter | solution.py:60
  813.1 227.6 %reduce-scatter.15.cloned.1.call-start = ((), (), s32[]{:S(2)}) async-start(), calls=%async_computation.16 | async-start | bytes 11141120 | tf_op jit(solution)/shard_map/reduce_scatter | solution.py:60
  841.3 221.9 %reduce-scatter.13.cloned.1.call-start = ((), (), s32[]{:S(2)}) async-start(), calls=%async_computation.15 | async-start | bytes 1572864 | tf_op jit(solution)/shard_map/reduce_scatter | solution.py:314
  862.2 387.9 %reduce-scatter.9.cloned.1.call-start = ((), (), s32[]{:S(2)}) async-start(), calls=%async_computation.11 | async-start | bytes 17301504 | tf_op jit(solution)/shard_map/reduce_scatter | solution.py:211
  883.5 369.7 %all-gather.24.cloned.1.call-start = ((), (), s32[]{:S(2)}) async-start(), calls=%async_computation.19 | async-start | bytes 2621440 | tf_op jit(solution)/shard_map/all_gather | solution.py:61
  945.2 312.3 %all-gather.22.cloned.1.call-start = ((), (), s32[]{:S(2)}) async-start(), calls=%async_computation.17 | async-start | bytes 3276800 | tf_op jit(solution)/shard_map/all_gather | solution.py:61
  1056.6 193.5 %copy-start.8 = (f32[256,1024]{1,0:T(8,128)S(1)}, f32[256,1024]{1,0:T(8,128)}, u32[]{:S(2)}) copy-start(f32[256,1024]{1,0:T(8,128)} %copy-done.6) | copy-start | bytes 3145732
  1056.6 193.5 %copy-start.21 = (bf16[256,1024]{1,0:T(8,128)(2,1)S(1)}, bf16[256,1024]{1,0:T(8,128)(2,1)}, u32[]{:S(2)}) copy-start(bf16[256,1024]{1,0:T(8,128)(2,1)} %param.18) | copy-start | bytes 1572868
  1056.6 193.5 %copy-start.22 = (bf16[256,1024]{1,0:T(8,128)(2,1)S(1)}, bf16[256,1024]{1,0:T(8,128)(2,1)}, u32[]{:S(2)}) copy-start(bf16[256,1024]{1,0:T(8,128)(2,1)} %reduce-scatter.11.cloned.1.call-done) | copy-start | bytes 1572868
  1056.6 193.5 %copy-start.51 = (f32[1024]{0:T(1024)S(1)}, f32[1024]{0:T(1024)}, u32[]{:S(2)}) copy-start(f32[1024]{0:T(1024)} %copy-done.49) | copy-start | bytes 12292
  1056.7 193.5 %copy-start.59 = (f32[256]{0:T(256)S(1)}, f32[256]{0:T(256)}, u32[]{:S(2)}) copy-start(f32[256]{0:T(256)} %copy-done.57) | copy-start | bytes 3076
  1056.7 193.5 %copy-start.68 = (f32[256]{0:T(256)S(1)}, f32[256]{0:T(256)}, u32[]{:S(2)}) copy-start(f32[256]{0:T(256)} %copy-done.67) | copy-start | bytes 3076
  (61 other events, 315.3 us)
Sparse Core Ops, SparseCore 0:
  15.0 139.7 all-reduce.6
  218.5 127.7 all-gather.17
  349.8 112.5 all-gather.15
  592.3 181.5 reduce-scatter.10
  945.3 36.6 all-gather.23
  1040.8 25.1 all-gather.21
Sparse Core Ops, SparseCore 1:
  16.9 23.8 all-gather.9
  43.5 88.4 all-gather.11
  134.5 72.7 all-gather.13
  214.8 30.8 reduce-scatter.6
  783.2 22.8 all-gather.19
  813.1 103.4 reduce-scatter.16
  920.5 120.0 reduce-scatter.14
  1043.3 19.9 reduce-scatter.12
  1065.4 184.6 reduce-scatter.8
